TPU v7x, 32 devices: a whole 2x2x4 slice. The times are simulated.
32 devices in a mesh: frame: 4 (over z), pipe: 4 (over x, core), dp: 2 (over y).
Axes of the slice: x: 2, y: 2, z: 4, core: 2. Of those that a mesh axis runs over, the one named last changes fastest.
Arguments:
- acts: bfloat16 [4, 2, 32, 4, 1280], P('pipe', 'dp', 'frame'), may hold values from -18 to 18
- cotangent: bfloat16 [4, 2, 32, 4, 1280], P('pipe', 'dp', 'frame'), may hold values from -6 to 6
- w_query: bfloat16 [4, 1280, 768], P('pipe'), may hold values from -0.15625 to 0.15625
- w_key: bfloat16 [4, 1280, 768], P('pipe'), may hold values from -0.15625 to 0.15625
- w_value: bfloat16 [4, 1280, 768], P('pipe'), may hold values from -0.15625 to 0.15625
- w_out: bfloat16 [4, 1280, 768], P('pipe'), may hold values from -0.21875 to 0.21875
Outputs:
- sent_grad: bfloat16 [4, 2, 32, 4, 1280], P('pipe', 'dp', 'frame')
- grad_value: float32 [4, 1280, 768], P('pipe', None, ('frame', 'dp'))
All inputs are finite; a program needn't handle non-finite values.
Results may differ from a plain program's by a relative error of at most 0.017.
The roundings to bfloat16 on the way count: a program that leaves them out, or rounds other values in their place, can miss the bound.
Values may be sent and summed in bfloat16 or wider, within the bound.
No kernel may reach another device: no remote copies, remote signals or barrier semaphores. Data moves between devices by JAX's collectives and lax.ppermute only.
A program may use at most 64 MiB of HBM per device.

v0:
```python
import jax
import jax.numpy as jnp
from jax import lax
from jax.sharding import PartitionSpec as P

HEADS = 12
HEAD_DIM = 64
score_scale = 0.125


def shifted(shard, axis, by):
    count = lax.axis_size(axis)
    pairs = [(i, i + by) for i in range(count) if 0 <= i + by < count]
    return lax.ppermute(shard, axis, pairs)


def attend_back(inputs, projected, w_query, w_key, w_value):
    frames = inputs.shape[0]
    places = inputs.shape[1]

    def project_heads(weight):
        result = jnp.dot(inputs, weight, preferred_element_type=jnp.float32).astype(jnp.bfloat16)
        return result.reshape(frames, places, HEADS, HEAD_DIM)

    queries = project_heads(w_query)
    key_rows = project_heads(w_key)
    values = project_heads(w_value)
    scores = (
        jnp.einsum("iphd,jphd->phij", queries, key_rows, preferred_element_type=jnp.float32)
        * score_scale
    )
    probability = jax.nn.softmax(scores, axis=-1)
    prob_short = probability.astype(jnp.bfloat16)
    proj_heads = projected.reshape(frames, places, HEADS, HEAD_DIM)
    grad_prob = jnp.einsum(
        "iphd,jphd->phij", proj_heads, values, preferred_element_type=jnp.float32
    )
    value_grad = jnp.einsum(
        "phij,iphd->jphd", prob_short, proj_heads, preferred_element_type=jnp.float32
    ).astype(jnp.bfloat16)
    score_grad = probability * (
        grad_prob - jnp.sum(grad_prob * probability, axis=-1, keepdims=True)
    )
    score_short = score_grad.astype(jnp.bfloat16)
    query_grad = (
        jnp.einsum("phij,jphd->iphd", score_short, key_rows, preferred_element_type=jnp.float32)
        * score_scale
    ).astype(jnp.bfloat16)
    key_grad = (
        jnp.einsum("phij,iphd->jphd", score_short, queries, preferred_element_type=jnp.float32)
        * score_scale
    ).astype(jnp.bfloat16)
    inner = HEADS * HEAD_DIM
    query_grad = query_grad.reshape(frames, places, inner)
    key_grad = key_grad.reshape(frames, places, inner)
    value_grad = value_grad.reshape(frames, places, inner)
    branch = jnp.einsum("fpj,cj->fpc", query_grad, w_query, preferred_element_type=jnp.float32)
    branch = branch + jnp.einsum("fpj,cj->fpc", key_grad, w_key, preferred_element_type=jnp.float32)
    branch = branch + jnp.einsum(
        "fpj,cj->fpc", value_grad, w_value, preferred_element_type=jnp.float32
    )
    branch = branch.astype(jnp.bfloat16)
    weight_grad = jnp.einsum("fpc,fpj->cj", inputs, value_grad, preferred_element_type=jnp.float32)
    return (branch, weight_grad)


def body(acts, cotangent, w_query, w_key, w_value, w_out):
    inputs = acts[0, 0]
    upstream = cotangent[0, 0]
    query_weight = w_query[0]
    key_weight = w_key[0]
    value_weight = w_value[0]
    out_weight = w_out[0]
    row_inputs, row_upstream = (
        lax.all_to_all(inputs, "frame", split_axis=1, concat_axis=0, tiled=True),
        lax.all_to_all(upstream, "frame", split_axis=1, concat_axis=0, tiled=True),
    )
    projected = jnp.dot(row_upstream, out_weight, preferred_element_type=jnp.float32).astype(
        jnp.bfloat16
    )
    branch, value_grad = attend_back(row_inputs, projected, query_weight, key_weight, value_weight)
    row_result = (row_upstream.astype(jnp.float32) + branch.astype(jnp.float32)).astype(
        jnp.bfloat16
    )
    frame_result = lax.all_to_all(row_result, "frame", split_axis=0, concat_axis=1, tiled=True)
    sent_grad = shifted(frame_result[None, None], "pipe", -1)
    value_middle = lax.psum_scatter(
        value_grad.astype(jnp.bfloat16), "frame", scatter_dimension=1, tiled=True
    )
    value_part = lax.psum_scatter(value_middle, "dp", scatter_dimension=1, tiled=True).astype(
        jnp.float32
    )
    return (sent_grad, value_part[None])


def solution(mesh):
    return jax.shard_map(
        body,
        mesh=mesh,
        in_specs=(
            P("pipe", "dp", "frame", None, None),
            P("pipe", "dp", "frame", None, None),
            P("pipe", None, None),
            P("pipe", None, None),
            P("pipe", None, None),
            P("pipe", None, None),
        ),
        out_specs=(P("pipe", "dp", "frame", None, None), P("pipe", None, ("frame", "dp"))),
        check_vma=False,
    )
```

profile of v0, /device:TPU:1, one launch (start us, length us, event | category | flops | bytes accessed | tf_op | source)
XLA Modules:
  0.0 102.3 jit_solution(5683003131072736057)
XLA Ops:
  7.2 1.7 %copy.98 = bf16[1,1,8,4,1280]{4,2,3,1,0:T(8,128)(2,1)} copy(bf16[1,1,8,4,1280]{4,3,2,1,0:T(4,128)(2,1)} %param.6) | data formatting | bytes 163840 | tf_op args[0]
  8.9 5.4 %all-to-all-start.1 = ((bf16[8,4,1280]{2,0,1:T(8,128)(2,1)}), bf16[8,4,1280]{2,0,1:T(8,128)(2,1)S(1)}, u32[]{:S(2)}, u32[]{:S(2)}) async-start(bf16[8,4,1280]{2,0,1:T(8,128)(2,1)} %bitcast.89), calls=%async_computation.1 | async-start | bytes 163840 | tf_op jit(solution)/shard_map/all_to_all | solution.py:75
  14.3 1.5 %copy.99 = bf16[1,1,8,4,1280]{4,2,3,1,0:T(8,128)(2,1)} copy(bf16[1,1,8,4,1280]{4,3,2,1,0:T(4,128)(2,1)} %param.7) | data formatting | bytes 163840 | tf_op args[1]
  15.8 3.1 %all-to-all-done.1 = bf16[8,4,1280]{2,0,1:T(8,128)(2,1)S(1)} async-done(((bf16[8,4,1280]{2,0,1:T(8,128)(2,1)}), bf16[8,4,1280]{2,0,1:T(8,128)(2,1)S(1)}, u32[]{:S(2)}, u32[]{:S(2)}) %all-to-all-start.1) | async-done | bytes 81952 | tf_op jit(solution)/shard_map/all_to_all | solution.py:75
  18.9 3.3 %all-to-all-start = ((bf16[8,4,1280]{2,0,1:T(8,128)(2,1)}), bf16[8,4,1280]{2,0,1:T(8,128)(2,1)S(1)}, u32[]{:S(2)}, u32[]{:S(2)}) async-start(bf16[8,4,1280]{2,0,1:T(8,128)(2,1)} %bitcast.90), calls=%async_computation | async-start | bytes 163840 | tf_op jit(solution)/shard_map/all_to_all | solution.py:76
  22.3 0.5 fusion.29
  22.7 1.1 %copy-done.1 = bf16[1,1280,768]{2,1,0:T(8,128)(2,1)S(1)} copy-done((bf16[1,1280,768]{2,1,0:T(8,128)(2,1)S(1)}, bf16[1,1280,768]{2,1,0:T(8,128)(2,1)}, u32[]{:S(2)}) %copy-start.1) | copy-done | bytes 1966104
  23.8 0.5 fusion.26
  24.6 2.2 %all-to-all-done = bf16[8,4,1280]{2,0,1:T(8,128)(2,1)S(1)} async-done(((bf16[8,4,1280]{2,0,1:T(8,128)(2,1)}), bf16[8,4,1280]{2,0,1:T(8,128)(2,1)S(1)}, u32[]{:S(2)}, u32[]{:S(2)}) %all-to-all-start) | async-done | bytes 81952 | tf_op jit(solution)/shard_map/all_to_all | solution.py:76
  26.8 2.0 %fusion.32 = bf16[32,768]{1,0:T(8,128)(2,1)S(1)} fusion(bf16[1,1280,768]{2,1,0:T(8,128)(2,1)} %param.11, bf16[8,4,1280]{2,0,1:T(8,128)(2,1)S(1)} %all-to-all-done), kind=kOutput, calls=%fused_computation.35 | convolution fusion | flops 62939136 | bytes 2097152 | tf_op jit(solution)/shard_map/dot_general | solution.py:78
  29.5 2.0 %fusion.1 = bf16[1280,768]{0,1:T(8,128)(2,1)} fusion(bf16[32,768]{1,0:T(8,128)(2,1)S(1)} %reshape.133, bf16[8,4,1280]{2,0,1:T(8,128)(2,1)S(1)} %all-to-all-done.1), kind=kOutput, calls=%fused_computation.2 | convolution fusion | flops 63897600 | bytes 2097152 | tf_op jit(solution)/shard_map/fpc,fpj->cj/dot_general | solution.py:63
  31.6 2.0 %fusion.35 = bf16[32,768]{1,0:T(8,128)(2,1)S(1)} fusion(bf16[1,1280,768]{2,1,0:T(8,128)(2,1)} %param.10, bf16[8,4,1280]{2,0,1:T(8,128)(2,1)S(1)} %all-to-all-done.1), kind=kOutput, calls=%fused_computation.36 | convolution fusion | flops 62939136 | bytes 2097152 | tf_op jit(solution)/shard_map/dot_general | solution.py:22
  34.8 39.4 %reduce-scatter.3.cloned.1.call-done = bf16[1280,192]{0,1:T(8,128)(2,1)} async-done(((bf16[1280,768]{0,1:T(8,128)(2,1)}), bf16[1280,192]{0,1:T(8,128)(2,1)}) %reduce-scatter.3.cloned.1.call-update) | async-done | bytes 491536 | tf_op jit(solution)/shard_map/reduce_scatter | solution.py:87
  74.2 0.7 fusion.12
  74.9 0.8 copy-done.2
  75.7 0.7 convolution_add_fusion.1
  76.4 0.7 fusion.6
  77.1 0.5 broadcast.23
  77.7 0.7 reduce.6
  78.4 7.6 %all_to_all.48 = bf16[4,2,5120]{2,1,0:T(2,128)(2,1)S(1)} all-to-all(bf16[4,2,5120]{2,1,0:T(2,128)(2,1)S(1)} %reshape.135), channel_id=1, replica_groups=mesh['frame'=4,'pipe'=4,'dp'=2] {'frame'}, dimensions={0} | all-to-all | bytes 163840 | tf_op jit(solution)/shard_map/all_to_all | solution.py:85
  86.1 3.9 %collective-permute-start = (bf16[1,1,8,4,1280]{4,2,3,1,0:T(8,128)(2,1)S(1)}, bf16[1,1,8,4,1280]{4,2,3,1,0:T(8,128)(2,1)S(1)}, u32[]{:S(2)}, u32[]{:S(2)}) collective-permute-start(bf16[1,1,8,4,1280]{4,2,3,1,0:T(8,128)(2,1)S(1)} %bitcast.91), channel_id=1, source_target_pairs={{2,0},{4,2},{6,4},{3,1},{5,3},{7,5},{10,8},{12,10},{14,12},{11,9},... | collective-permute-start | bytes 245768 | tf_op jit(solution)/shard_map/ppermute | solution.py:14
  90.0 3.0 %collective-permute-done = bf16[1,1,8,4,1280]{4,2,3,1,0:T(8,128)(2,1)S(1)} collective-permute-done((bf16[1,1,8,4,1280]{4,2,3,1,0:T(8,128)(2,1)S(1)}, bf16[1,1,8,4,1280]{4,2,3,1,0:T(8,128)(2,1)S(1)}, u32[]{:S(2)}, u32[]{:S(2)}) %collective-permute-start) | collective-permute-done | bytes 81952 | tf_op jit(solution)/shard_map/ppermute | solution.py:14
  93.0 0.7 copy.61
  93.7 1.8 %bitcast_convert_fusion = f32[1,1280,96]{1,2,0:T(8,128)} fusion(bf16[1280,96]{0,1:T(8,128)(2,1)} %reduce-scatter.5.cloned.1.call-done), kind=kLoop, calls=%fused_computation.37 | loop fusion | flops 122880 | bytes 737280 | tf_op jit(solution)/shard_map/broadcast_in_dim | solution.py:93
  (30 shorter events, 2.4 us)
Async XLA Ops:
  7.2 15.1 %copy-start = (bf16[1,1280,768]{2,1,0:T(8,128)(2,1)S(1)}, bf16[1,1280,768]{2,1,0:T(8,128)(2,1)}, u32[]{:S(2)}) copy-start(bf16[1,1280,768]{2,1,0:T(8,128)(2,1)} %param.8) | copy-start | bytes 5898244
  8.9 10.0 %all-to-all-start.1 = ((bf16[8,4,1280]{2,0,1:T(8,128)(2,1)}), bf16[8,4,1280]{2,0,1:T(8,128)(2,1)S(1)}, u32[]{:S(2)}, u32[]{:S(2)}) async-start(bf16[8,4,1280]{2,0,1:T(8,128)(2,1)} %bitcast.89), calls=%async_computation.1 | async-start | bytes 163840 | tf_op jit(solution)/shard_map/all_to_all | solution.py:75
  18.9 7.9 %all-to-all-start = ((bf16[8,4,1280]{2,0,1:T(8,128)(2,1)}), bf16[8,4,1280]{2,0,1:T(8,128)(2,1)S(1)}, u32[]{:S(2)}, u32[]{:S(2)}) async-start(bf16[8,4,1280]{2,0,1:T(8,128)(2,1)} %bitcast.90), calls=%async_computation | async-start | bytes 163840 | tf_op jit(solution)/shard_map/all_to_all | solution.py:76
  22.2 51.9 %reduce-scatter.3.cloned.1.call-start = ((), (), s32[]{:S(2)}) async-start(), calls=%async_computation.5 | async-start | bytes 2457600 | tf_op jit(solution)/shard_map/reduce_scatter | solution.py:87
  22.3 1.5 %copy-start.1 = (bf16[1,1280,768]{2,1,0:T(8,128)(2,1)S(1)}, bf16[1,1280,768]{2,1,0:T(8,128)(2,1)}, u32[]{:S(2)}) copy-start(bf16[1,1280,768]{2,1,0:T(8,128)(2,1)} %param.9) | copy-start | bytes 5898244
  31.5 62.2 %reduce-scatter.5.cloned.1.call-start = ((), (), s32[]{:S(2)}) async-start(), calls=%async_computation.6 | async-start | bytes 737280 | tf_op jit(solution)/shard_map/reduce_scatter | solution.py:90
  74.2 1.5 %copy-start.2 = (bf16[1,1280,768]{2,1,0:T(8,128)(2,1)S(1)}, bf16[1,1280,768]{2,1,0:T(8,128)(2,1)}, u32[]{:S(2)}) copy-start(bf16[1,1280,768]{2,1,0:T(8,128)(2,1)} %param.9) | copy-start | bytes 5898244
  74.2 2.2 %copy-start.3 = (bf16[1,1280,768]{2,1,0:T(8,128)(2,1)S(1)}, bf16[1,1280,768]{2,1,0:T(8,128)(2,1)}, u32[]{:S(2)}) copy-start(bf16[1,1280,768]{2,1,0:T(8,128)(2,1)} %param.10) | copy-start | bytes 5898244
  86.1 6.9 %collective-permute-start = (bf16[1,1,8,4,1280]{4,2,3,1,0:T(8,128)(2,1)S(1)}, bf16[1,1,8,4,1280]{4,2,3,1,0:T(8,128)(2,1)S(1)}, u32[]{:S(2)}, u32[]{:S(2)}) collective-permute-start(bf16[1,1,8,4,1280]{4,2,3,1,0:T(8,128)(2,1)S(1)} %bitcast.91), channel_id=1, source_target_pairs={{2,0},{4,2},{6,4},{3,1},{5,3},{7,5},{10,8},{12,10},{14,12},{11,9},... | collective-permute-start | bytes 245768 | tf_op jit(solution)/shard_map/ppermute | solution.py:14
Sparse Core Ops, SparseCore 0:
  31.7 42.4 reduce-scatter.2
  76.4 13.5 reduce-scatter.4
where the time goes:
time: 103 us; the launch traced here: 102 us
  waiting for transfers between devices  47.8 us (46%)
  between operations  14.2 us (14%)
  starting transfers between devices  12.7 us (12%)
  matrix products  9.96 us (10%)
  blocking collectives  7.64 us (7%)
  local copies, waits for them, and re-layouts  7.55 us (7%)
  other arithmetic  2.47 us (2%)
    reduce_scatter x1, waiting for transfers between devices, body(): lax.psum_scatter(value_grad.astype(jnp.bfloat16), 'frame', scatter_dimens...  39.4 us
    all_to_all x1, blocking collectives, body(): lax.all_to_all(row_result, 'frame', split_axis=0, concat_axis=1, tiled=True)  7.64 us
    unnamed x14, local copies, waits for them, and re-layouts  5.91 us
    all_to_all x1, starting transfers between devices, body(): lax.all_to_all(inputs, 'frame', split_axis=1, concat_axis=0, tiled=True)  5.41 us
    ppermute x1, starting transfers between devices, shifted(): return lax.ppermute(shard, axis, pairs)  3.88 us
    all_to_all x1, starting transfers between devices, body(): lax.all_to_all(upstream, 'frame', split_axis=1, concat_axis=0, tiled=True)  3.3 us
    all_to_all x1, waiting for transfers between devices, body(): lax.all_to_all(inputs, 'frame', split_axis=1, concat_axis=0, tiled=True)  3.11 us
    ppermute x1, waiting for transfers between devices, shifted(): return lax.ppermute(shard, axis, pairs)  3.04 us
  transfers between devices with their start and end apart: 5, of which 4 were waited for; matrix products, arithmetic and copies ran while one was open for 10% of the time, Pallas kernels for 0%

commit v1 on v0

--- a/solution.py
+++ b/solution.py
@@ -6,6 +6,17 @@
 HEADS = 12
 HEAD_DIM = 64
 score_scale = 0.125
+
+
+def cut_along(x, dim, count):
+    before, after = (x.shape[:dim], x.shape[dim + 1 :])
+    return jnp.moveaxis(x.reshape(*before, count, -1, *after), dim, 0)
+
+
+def laid_out(blocks, dim):
+    shape = list(blocks.shape[1:])
+    shape[dim] *= blocks.shape[0]
+    return jnp.moveaxis(blocks, 0, dim).reshape(shape)
 
 
 def shifted(shard, axis, by):
@@ -82,7 +93,14 @@
     row_result = (row_upstream.astype(jnp.float32) + branch.astype(jnp.float32)).astype(
         jnp.bfloat16
     )
-    frame_result = lax.all_to_all(row_result, "frame", split_axis=0, concat_axis=1, tiled=True)
+    devices, here = (lax.axis_size("frame"), lax.axis_index("frame"))
+    pieces = cut_along(row_result, 0, devices)
+    outs = [pieces[here]]
+    for turn in range(1, devices):
+        sent = pieces[here ^ turn]
+        outs.append(lax.ppermute(sent, "frame", [(i_2, i_2 ^ turn) for i_2 in range(devices)]))
+    pieces = jnp.stack(outs)[here ^ jnp.arange(devices)]
+    frame_result = laid_out(pieces, 1)
     sent_grad = shifted(frame_result[None, None], "pipe", -1)
     value_middle = lax.psum_scatter(
         value_grad.astype(jnp.bfloat16), "frame", scatter_dimension=1, tiled=True

time: 103 us -> 100 us (0.971)
  blocking collectives: 7.64 us -> 0 us
  starting transfers between devices: 12.7 us -> 16.8 us
  matrix products: 9.96 us -> 11.7 us
    all_to_all x1 -> x0, blocking collectives: 7.64 us -> none  [body(): lax.all_to_all(row_result, 'frame', split_axis=0, concat_axis=1, tiled=True)]
    ppermute x0 -> x3, starting transfers between devices: none -> 3.61 us  [body(): lax.ppermute(sent, 'frame', [(i_2, i_2 ^ turn) for i_2 in range(devices)])]
    dot_general x1, matrix products: 0.7 us -> 2.39 us  [attend_back(): jnp.einsum('fpj,cj->fpc', key_grad, w_key, preferred_element_type=jnp.flo...]
    ppermute x0 -> x3, waiting for transfers between devices: none -> 1.39 us  [body(): lax.ppermute(sent, 'frame', [(i_2, i_2 ^ turn) for i_2 in range(devices)])]
    unnamed x14 -> x9, local copies, waits for them, and re-layouts: 5.91 us -> 4.97 us
  transfers between devices with their start and end apart: 5 -> 8, of which waited for: 4 -> 6; matrix products, arithmetic and copies ran while one was open for 10% -> 11% of each run, Pallas kernels for 0% -> 0%
where the time goes in v1:
time: 100 us; the launch traced here: 99.8 us
  waiting for transfers between devices  48.6 us (49%)
  starting transfers between devices  16.8 us (17%)
  between operations  14.2 us (14%)
  matrix products  11.7 us (12%)
  local copies, waits for them, and re-layouts  6.65 us (7%)
  other arithmetic  1.83 us (2%)
    reduce_scatter x1, waiting for transfers between devices, body(): lax.psum_scatter(value_grad.astype(jnp.bfloat16), 'frame', scatter_dimens...  38.6 us
    all_to_all x1, starting transfers between devices, body(): lax.all_to_all(inputs, 'frame', split_axis=1, concat_axis=0, tiled=True)  5.41 us
    unnamed x9, local copies, waits for them, and re-layouts  4.97 us
    ppermute x1, starting transfers between devices, shifted(): return lax.ppermute(shard, axis, pairs)  4.42 us
    ppermute x3, starting transfers between devices, body(): lax.ppermute(sent, 'frame', [(i_2, i_2 ^ turn) for i_2 in range(devices)])  3.61 us
    all_to_all x1, starting transfers between devices, body(): lax.all_to_all(upstream, 'frame', split_axis=1, concat_axis=0, tiled=True)  3.3 us
    ppermute x1, waiting for transfers between devices, shifted(): return lax.ppermute(shard, axis, pairs)  3.17 us
    all_to_all x1, waiting for transfers between devices, body(): lax.all_to_all(inputs, 'frame', split_axis=1, concat_axis=0, tiled=True)  3.11 us
  transfers between devices with their start and end apart: 8, of which 6 were waited for; matrix products, arithmetic and copies ran while one was open for 11% of the time, Pallas kernels for 0%

profile of v1, /device:TPU:1, one launch (start us, length us, event | category | flops | bytes accessed | tf_op | source)
XLA Modules:
  0.0 99.8 jit_solution(3172736112007728125)
XLA Ops:
  7.2 1.7 %copy.78 = bf16[1,1,8,4,1280]{4,2,3,1,0:T(8,128)(2,1)} copy(bf16[1,1,8,4,1280]{4,3,2,1,0:T(4,128)(2,1)} %param.6) | data formatting | bytes 163840 | tf_op args[0]
  8.9 5.4 %all-to-all-start.1 = ((bf16[8,4,1280]{2,0,1:T(8,128)(2,1)}), bf16[8,4,1280]{2,0,1:T(8,128)(2,1)S(1)}, u32[]{:S(2)}, u32[]{:S(2)}) async-start(bf16[8,4,1280]{2,0,1:T(8,128)(2,1)} %bitcast.100), calls=%async_computation.1 | async-start | bytes 163840 | tf_op jit(solution)/shard_map/all_to_all | solution.py:86
  14.3 1.5 %copy.79 = bf16[1,1,8,4,1280]{4,2,3,1,0:T(8,128)(2,1)} copy(bf16[1,1,8,4,1280]{4,3,2,1,0:T(4,128)(2,1)} %param.7) | data formatting | bytes 163840 | tf_op args[1]
  15.8 3.1 %all-to-all-done.1 = bf16[8,4,1280]{2,0,1:T(8,128)(2,1)S(1)} async-done(((bf16[8,4,1280]{2,0,1:T(8,128)(2,1)}), bf16[8,4,1280]{2,0,1:T(8,128)(2,1)S(1)}, u32[]{:S(2)}, u32[]{:S(2)}) %all-to-all-start.1) | async-done | bytes 81952 | tf_op jit(solution)/shard_map/all_to_all | solution.py:86
  18.9 3.3 %all-to-all-start = ((bf16[8,4,1280]{2,0,1:T(8,128)(2,1)}), bf16[8,4,1280]{2,0,1:T(8,128)(2,1)S(1)}, u32[]{:S(2)}, u32[]{:S(2)}) async-start(bf16[8,4,1280]{2,0,1:T(8,128)(2,1)} %bitcast.101), calls=%async_computation | async-start | bytes 163840 | tf_op jit(solution)/shard_map/all_to_all | solution.py:87
  22.3 0.5 fusion.29
  22.7 1.1 %copy-done.1 = bf16[1,1280,768]{2,1,0:T(8,128)(2,1)S(1)} copy-done((bf16[1,1280,768]{2,1,0:T(8,128)(2,1)S(1)}, bf16[1,1280,768]{2,1,0:T(8,128)(2,1)}, u32[]{:S(2)}) %copy-start.1) | copy-done | bytes 1966104
  24.6 2.2 %all-to-all-done = bf16[8,4,1280]{2,0,1:T(8,128)(2,1)S(1)} async-done(((bf16[8,4,1280]{2,0,1:T(8,128)(2,1)}), bf16[8,4,1280]{2,0,1:T(8,128)(2,1)S(1)}, u32[]{:S(2)}, u32[]{:S(2)}) %all-to-all-start) | async-done | bytes 81952 | tf_op jit(solution)/shard_map/all_to_all | solution.py:87
  26.8 2.0 %fusion.32 = bf16[32,768]{1,0:T(8,128)(2,1)S(1)} fusion(bf16[1,1280,768]{2,1,0:T(8,128)(2,1)} %param.11, bf16[8,4,1280]{2,0,1:T(8,128)(2,1)S(1)} %all-to-all-done), kind=kOutput, calls=%fused_computation.36 | convolution fusion | flops 62939136 | bytes 2097152 | tf_op jit(solution)/shard_map/dot_general | solution.py:89
  29.5 2.0 %fusion.1 = bf16[1280,768]{0,1:T(8,128)(2,1)} fusion(bf16[32,768]{1,0:T(8,128)(2,1)S(1)} %reshape.152, bf16[8,4,1280]{2,0,1:T(8,128)(2,1)S(1)} %all-to-all-done.1), kind=kOutput, calls=%fused_computation.3 | convolution fusion | flops 63897600 | bytes 2097152 | tf_op jit(solution)/shard_map/fpc,fpj->cj/dot_general | solution.py:74
  31.6 2.0 %fusion.35 = bf16[32,768]{1,0:T(8,128)(2,1)S(1)} fusion(bf16[1,1280,768]{2,1,0:T(8,128)(2,1)} %param.10, bf16[8,4,1280]{2,0,1:T(8,128)(2,1)S(1)} %all-to-all-done.1), kind=kOutput, calls=%fused_computation.37 | convolution fusion | flops 62939136 | bytes 2097152 | tf_op jit(solution)/shard_map/dot_general | solution.py:33
  34.8 0.7 fusion.12
  35.5 38.6 %reduce-scatter.3.cloned.1.call-done = bf16[1280,192]{0,1:T(8,128)(2,1)} async-done(((bf16[1280,768]{0,1:T(8,128)(2,1)}), bf16[1280,192]{0,1:T(8,128)(2,1)}) %reduce-scatter.3.cloned.1.call-update) | async-done | bytes 491536 | tf_op jit(solution)/shard_map/reduce_scatter | solution.py:105
  74.2 2.4 %convolution_add_fusion.1 = f32[32,1280]{1,0:T(8,128)S(1)} fusion(f32[32,1280]{1,0:T(8,128)S(1)} %fusion.12, bf16[32,768]{1,0:T(8,128)(2,1)S(1)} %reshape.151, bf16[1,1280,768]{2,1,0:T(8,128)(2,1)} %param.9), kind=kOutput, calls=%fused_computation.5 | convolution fusion | flops 62955520 | bytes 2342912 | tf_op jit(solution)/shard_map/fpj,cj->fpc/dot_general | solution.py:69
  76.6 0.7 fusion.6
  77.3 1.5 %collective-permute-start.2 = (bf16[8,1,1280]{2,0,1:T(8,128)(2,1)S(1)}, bf16[8,1,1280]{2,0,1:T(8,128)(2,1)S(1)}, u32[]{:S(2)}, u32[]{:S(2)}) collective-permute-start(bf16[8,1,1280]{2,0,1:T(8,128)(2,1)S(1)} %get-tuple-element.7), channel_id=1, source_target_pairs={{0,24},{8,16},{16,8},{24,0},{1,25},{9,17},{17,9},{25,1},{2,26},{10... | collective-permute-start | bytes 61448 | tf_op jit(solution)/shard_map/ppermute | solution.py:101
  79.1 1.9 %collective-permute-start = (bf16[8,1,1280]{2,0,1:T(8,128)(2,1)S(1)}, bf16[8,1,1280]{2,0,1:T(8,128)(2,1)S(1)}, u32[]{:S(2)}, u32[]{:S(2)}) collective-permute-start(bf16[8,1,1280]{2,0,1:T(8,128)(2,1)S(1)} %get-tuple-element.9), channel_id=1, source_target_pairs={{0,8},{8,0},{16,24},{24,16},{1,9},{9,1},{17,25},{25,17},{2,10},{10... | collective-permute-start | bytes 61448 | tf_op jit(solution)/shard_map/ppermute | solution.py:101
  81.0 0.9 collective-permute-done.2
  81.8 0.5 collective-permute-done.1
  82.4 0.6 gather_fusion
  82.9 4.4 %collective-permute-start.3 = (bf16[1,1,8,4,1280]{4,2,3,1,0:T(8,128)(2,1)S(1)}, bf16[1,1,8,4,1280]{4,2,3,1,0:T(8,128)(2,1)S(1)}, u32[]{:S(2)}, u32[]{:S(2)}) collective-permute-start(bf16[1,1,8,4,1280]{4,2,3,1,0:T(8,128)(2,1)S(1)} %bitcast.102), channel_id=1, source_target_pairs={{2,0},{4,2},{6,4},{3,1},{5,3},{7,5},{10,8},{12,10},{14,12},{11,9},... | collective-permute-start | bytes 245768 | tf_op jit(solution)/shard_map/ppermute | solution.py:25
  87.4 3.2 %collective-permute-done.3 = bf16[1,1,8,4,1280]{4,2,3,1,0:T(8,128)(2,1)S(1)} collective-permute-done((bf16[1,1,8,4,1280]{4,2,3,1,0:T(8,128)(2,1)S(1)}, bf16[1,1,8,4,1280]{4,2,3,1,0:T(8,128)(2,1)S(1)}, u32[]{:S(2)}, u32[]{:S(2)}) %collective-permute-start.3) | collective-permute-done | bytes 81952 | tf_op jit(solution)/shard_map/ppermute | solution.py:25
  90.5 0.7 copy.44
  91.2 1.8 %bitcast_convert_fusion = f32[1,1280,96]{1,2,0:T(8,128)} fusion(bf16[1280,96]{0,1:T(8,128)(2,1)} %reduce-scatter.5.cloned.1.call-done), kind=kLoop, calls=%fused_computation.38 | loop fusion | flops 122880 | bytes 737280 | tf_op jit(solution)/shard_map/broadcast_in_dim | solution.py:111
  (33 shorter events, 3.0 us)
Async XLA Ops:
  7.2 15.1 %copy-start = (bf16[1,1280,768]{2,1,0:T(8,128)(2,1)S(1)}, bf16[1,1280,768]{2,1,0:T(8,128)(2,1)}, u32[]{:S(2)}) copy-start(bf16[1,1280,768]{2,1,0:T(8,128)(2,1)} %param.8) | copy-start | bytes 5898244
  8.9 10.0 %all-to-all-start.1 = ((bf16[8,4,1280]{2,0,1:T(8,128)(2,1)}), bf16[8,4,1280]{2,0,1:T(8,128)(2,1)S(1)}, u32[]{:S(2)}, u32[]{:S(2)}) async-start(bf16[8,4,1280]{2,0,1:T(8,128)(2,1)} %bitcast.100), calls=%async_computation.1 | async-start | bytes 163840 | tf_op jit(solution)/shard_map/all_to_all | solution.py:86
  18.9 7.9 %all-to-all-start = ((bf16[8,4,1280]{2,0,1:T(8,128)(2,1)}), bf16[8,4,1280]{2,0,1:T(8,128)(2,1)S(1)}, u32[]{:S(2)}, u32[]{:S(2)}) async-start(bf16[8,4,1280]{2,0,1:T(8,128)(2,1)} %bitcast.101), calls=%async_computation | async-start | bytes 163840 | tf_op jit(solution)/shard_map/all_to_all | solution.py:87
  22.2 52.0 %reduce-scatter.3.cloned.1.call-start = ((), (), s32[]{:S(2)}) async-start(), calls=%async_computation.4 | async-start | bytes 2457600 | tf_op jit(solution)/shard_map/reduce_scatter | solution.py:105
  22.3 1.5 %copy-start.1 = (bf16[1,1280,768]{2,1,0:T(8,128)(2,1)S(1)}, bf16[1,1280,768]{2,1,0:T(8,128)(2,1)}, u32[]{:S(2)}) copy-start(bf16[1,1280,768]{2,1,0:T(8,128)(2,1)} %param.9) | copy-start | bytes 5898244
  31.6 59.6 %reduce-scatter.5.cloned.1.call-start = ((), (), s32[]{:S(2)}) async-start(), calls=%async_computation.5 | async-start | bytes 737280 | tf_op jit(solution)/shard_map/reduce_scatter | solution.py:108
  74.2 2.4 %copy-start.2 = (bf16[1,1280,768]{2,1,0:T(8,128)(2,1)S(1)}, bf16[1,1280,768]{2,1,0:T(8,128)(2,1)}, u32[]{:S(2)}) copy-start(bf16[1,1280,768]{2,1,0:T(8,128)(2,1)} %param.10) | copy-start | bytes 5898244
  77.3 4.5 %collective-permute-start.2 = (bf16[8,1,1280]{2,0,1:T(8,128)(2,1)S(1)}, bf16[8,1,1280]{2,0,1:T(8,128)(2,1)S(1)}, u32[]{:S(2)}, u32[]{:S(2)}) collective-permute-start(bf16[8,1,1280]{2,0,1:T(8,128)(2,1)S(1)} %get-tuple-element.7), channel_id=1, source_target_pairs={{0,24},{8,16},{16,8},{24,0},{1,25},{9,17},{17,9},{25,1},{2,26},{10... | collective-permute-start | bytes 61448 | tf_op jit(solution)/shard_map/ppermute | solution.py:101
  78.8 3.5 %collective-permute-start.1 = (bf16[8,1,1280]{2,0,1:T(8,128)(2,1)S(1)}, bf16[8,1,1280]{2,0,1:T(8,128)(2,1)S(1)}, u32[]{:S(2)}, u32[]{:S(2)}) collective-permute-start(bf16[8,1,1280]{2,0,1:T(8,128)(2,1)S(1)} %get-tuple-element.8), channel_id=1, source_target_pairs={{0,16},{8,24},{16,0},{24,8},{1,17},{9,25},{17,1},{25,9},{2,18},{10... | collective-permute-start | bytes 61448 | tf_op jit(solution)/shard_map/ppermute | solution.py:101
  79.1 3.3 %collective-permute-start = (bf16[8,1,1280]{2,0,1:T(8,128)(2,1)S(1)}, bf16[8,1,1280]{2,0,1:T(8,128)(2,1)S(1)}, u32[]{:S(2)}, u32[]{:S(2)}) collective-permute-start(bf16[8,1,1280]{2,0,1:T(8,128)(2,1)S(1)} %get-tuple-element.9), channel_id=1, source_target_pairs={{0,8},{8,0},{16,24},{24,16},{1,9},{9,1},{17,25},{25,17},{2,10},{10... | collective-permute-start | bytes 61448 | tf_op jit(solution)/shard_map/ppermute | solution.py:101
  82.9 7.6 %collective-permute-start.3 = (bf16[1,1,8,4,1280]{4,2,3,1,0:T(8,128)(2,1)S(1)}, bf16[1,1,8,4,1280]{4,2,3,1,0:T(8,128)(2,1)S(1)}, u32[]{:S(2)}, u32[]{:S(2)}) collective-permute-start(bf16[1,1,8,4,1280]{4,2,3,1,0:T(8,128)(2,1)S(1)} %bitcast.102), channel_id=1, source_target_pairs={{2,0},{4,2},{6,4},{3,1},{5,3},{7,5},{10,8},{12,10},{14,12},{11,9},... | collective-permute-start | bytes 245768 | tf_op jit(solution)/shard_map/ppermute | solution.py:25
Sparse Core Ops, SparseCore 0:
  31.7 42.4 reduce-scatter.2
  76.4 13.5 reduce-scatter.4
